TPU v7x, 256 devices: a whole 4x4x8 slice. The times are simulated.
256 devices in a mesh: gx: 8 (over x, core), gy: 4 (over y), gz: 8 (over z).
Axes of the slice: x: 4, y: 4, z: 8, core: 2. Of those that a mesh axis runs over, the one named last changes fastest.
Arguments:
- left_core: float32 [256, 4096, 256], P(None, ('gx', 'gy', 'gz')), may hold values from -4000 to 4000
- right_core: float32 [256, 4096, 256], P(None, ('gx', 'gy', 'gz')), may hold values from -0.00012207031 to 0.00012207031
Outputs:
- left_out: float32 [256, 4096, 128], P(None, ('gx', 'gy', 'gz'))
- right_out: float32 [128, 4096, 256], P(None, ('gx', 'gy', 'gz'))
- next_factor: float32 [256, 256], replicated
All inputs are finite; a program needn't handle non-finite values.
Results may differ from a plain program's by a relative error of at most 0.000075.
Values sent between devices are 32-bit elements; how exact they have to be, the bound alone decides.
A program may use at most 192 MiB of HBM per device.

v0:
```python
import math
import jax
import jax.numpy as jnp
from jax import lax
from jax.sharding import PartitionSpec as P

RK = 128


def gram_of(matrix_rows):
    return lax.dot_general(
        matrix_rows,
        matrix_rows,
        (((0,), (0,)), ((), ())),
        precision=lax.Precision.HIGHEST,
        preferred_element_type=jnp.float32,
    )


def per_device(left_core, right_core):
    rank_left, points_local, rank_mid = left_core.shape
    rank_right = right_core.shape[2]
    total_points = points_local * lax.axis_size("gx") * lax.axis_size("gy") * lax.axis_size("gz")
    unfold = left_core.reshape(rank_left * points_local, rank_mid)
    lower_one = jnp.linalg.cholesky(lax.psum(gram_of(unfold), ("gx", "gy", "gz")))
    upper_full = lower_one.T
    ortho_cols = lax.linalg.triangular_solve(
        lower_one[:RK, :RK], unfold[:, :RK], left_side=False, lower=True, transpose_a=True
    )
    left_out = (ortho_cols * math.sqrt(rank_left * total_points)).reshape(
        rank_left, points_local, RK
    )
    absorbed = jnp.dot(
        upper_full[:RK, :],
        right_core.reshape(rank_mid, points_local * rank_right),
        precision=lax.Precision.HIGHEST,
        preferred_element_type=jnp.float32,
    )
    summed = lax.psum(gram_of(absorbed.reshape(RK * points_local, rank_right)), ("gx", "gy", "gz"))
    factor = jnp.linalg.cholesky(summed / (RK * total_points)).T
    right_out = absorbed.reshape(RK, points_local, rank_right)
    return (left_out, right_out, factor)


def solution(mesh):
    in_specs = (P(None, ("gx", "gy", "gz"), None), P(None, ("gx", "gy", "gz"), None))
    out_specs = (P(None, ("gx", "gy", "gz"), None), P(None, ("gx", "gy", "gz"), None), P())
    return jax.shard_map(
        per_device, mesh=mesh, in_specs=in_specs, out_specs=out_specs, check_vma=False
    )
```

profile of v0, /device:TPU:2, one launch (start us, length us, event | category | flops | bytes accessed | tf_op | source)
XLA Modules:
  0.0 617.6 jit_solution(7845188268302011180)
XLA Ops:
  7.2 0.0 all-reduce.4.cloned.1.call-start
  7.2 10.9 %convolution_bitcast_fusion = f32[256,256]{0,1:T(8,128)} fusion(f32[256,16,256]{2,1,0:T(8,128)} %param.3), kind=kOutput, calls=%fused_computation.3 | convolution fusion | flops 3221225472 | bytes 4456448 | tf_op jit(solution)/shard_map/dot_general | solution.py:11
  18.1 0.0 all-reduce.4.cloned.1.call-update
  18.1 0.5 all-reduce.6.cloned.1.call-start
  18.6 7.9 %copy.26 = f32[32,8,16,256]{3,1,2,0:T(8,128)} copy(f32[32,8,16,256]{3,2,1,0:T(8,128)} %bitcast.53) | data formatting | bytes 8388608
  26.5 244.9 %all-reduce.4.cloned.1.call-done = f32[256,256]{0,1:T(8,128)} async-done(((f32[256,256]{0,1:T(8,128)}), f32[256,256]{0,1:T(8,128)}) %all-reduce.4.cloned.1.call-update) | async-done | bytes 262160 | tf_op jit(solution)/shard_map/psum | solution.py:25
  271.5 1.1 copy.16
  272.6 1.0 fusion.3
  273.6 11.7 %cholesky.130 = f32[128,128]{1,0:T(8,128)S(1)} custom-call(f32[128,128]{1,0:T(8,128)S(1)} %cholesky.194), custom_call_target="Cholesky" | custom-call | tf_op jit(solution)/shard_map/jit(cholesky)/cholesky | solution.py:25
  285.3 9.8 %custom-call.13 = f32[1,128,128]{1,2,0:T(8,128)S(1)} custom-call(f32[1,128,128]{2,1,0:T(8,128)S(1)} %get-tuple-element.17), custom_call_target="InvertDiagBlocksLowerTriangular" | custom-call | tf_op jit(solution)/shard_map/jit(cholesky)/cholesky | solution.py:25
  295.2 0.2 constant_dynamic-update-slice_fusion.3
  295.4 0.3 convolution_subtract_fusion.1
  295.6 11.9 %cholesky.147 = f32[128,128]{1,0:T(8,128)S(1)} custom-call(f32[128,128]{1,0:T(8,128)S(1)} %convolution_subtract_fusion.1), custom_call_target="Cholesky" | custom-call | tf_op jit(solution)/shard_map/jit(cholesky)/cholesky | solution.py:25
  307.5 0.6 compare_reduce_fusion.2
  309.6 4.5 fusion.4
  314.1 1.5 reshape.39
  315.5 6.4 %fusion.14 = f32[256,256]{0,1:T(8,128)} fusion(f32[2048,256]{1,0:T(8,128)} %reshape.39), kind=kOutput, calls=%fused_computation.41 | convolution fusion | flops 1610612736 | bytes 2359296 | tf_op jit(solution)/shard_map/dot_general | solution.py:11
  321.9 0.0 all-reduce.6.cloned.1.call-update
  322.0 9.8 %custom-call.11 = f32[1,128,128]{1,2,0:T(8,128)S(1)} custom-call(f32[1,128,128]{2,1,0:T(8,128)S(1)} %fusion.8), custom_call_target="InvertDiagBlocksLowerTriangular" | custom-call | tf_op jit(solution)/shard_map/triangular_solve | solution.py:27
  331.8 4.9 fusion
  336.7 2.0 copy.27
  338.6 3.1 copy.17
  341.7 229.4 %all-reduce.6.cloned.1.call-done = f32[256,256]{0,1:T(8,128)} async-done(((f32[256,256]{0,1:T(8,128)}), f32[256,256]{0,1:T(8,128)}) %all-reduce.6.cloned.1.call-update) | async-done | bytes 262160 | tf_op jit(solution)/shard_map/psum | solution.py:39
  571.1 1.0 broadcast_multiply_fusion
  572.0 0.1 copy.19
  572.2 1.0 fusion.2
  573.2 11.7 %cholesky.164 = f32[128,128]{1,0:T(8,128)S(1)} custom-call(f32[128,128]{1,0:T(8,128)S(1)} %cholesky.197), custom_call_target="Cholesky" | custom-call | tf_op jit(solution)/shard_map/jit(cholesky)/cholesky | solution.py:40
  585.0 9.8 %custom-call.14 = f32[1,128,128]{1,2,0:T(8,128)S(1)} custom-call(f32[1,128,128]{2,1,0:T(8,128)S(1)} %get-tuple-element.13), custom_call_target="InvertDiagBlocksLowerTriangular" | custom-call | tf_op jit(solution)/shard_map/jit(cholesky)/cholesky | solution.py:40
  594.8 0.2 constant_dynamic-update-slice_fusion.1
  595.0 0.3 convolution_subtract_fusion
  595.3 11.7 %cholesky.181 = f32[128,128]{1,0:T(8,128)S(1)} custom-call(f32[128,128]{1,0:T(8,128)S(1)} %convolution_subtract_fusion), custom_call_target="Cholesky" | custom-call | tf_op jit(solution)/shard_map/jit(cholesky)/cholesky | solution.py:40
  607.0 0.7 compare_reduce_fusion
  607.7 0.6 compare_reduce_fusion.1
  609.7 0.8 copy.20
  (12 shorter events, 0.3 us)
Async XLA Ops:
  7.2 264.3 %all-reduce.4.cloned.1.call-start = ((), (), s32[]{:S(2)}) async-start(), calls=%async_computation | async-start | bytes 524288 | tf_op jit(solution)/shard_map/psum | solution.py:25
  18.1 552.9 %all-reduce.6.cloned.1.call-start = ((), (), s32[]{:S(2)}) async-start(), calls=%async_computation.1 | async-start | bytes 524288 | tf_op jit(solution)/shard_map/psum | solution.py:39
Sparse Core Ops, SparseCore 0:
  18.2 253.1 all-reduce.3
  322.1 248.9 all-reduce.5
where the time goes:
time: 623 us; the launch traced here: 618 us
  waiting for transfers between devices  474 us (76%)
  other arithmetic  81.6 us (13%)
  matrix products  27.6 us (4%)
  between operations  17.1 us (3%)
  local copies, waits for them, and re-layouts  16.5 us (3%)
    psum x1, waiting for transfers between devices, per_device(): lax.psum(gram_of(unfold), ('gx', 'gy', 'gz'))  245 us
    psum x1, waiting for transfers between devices, per_device(): lax.psum(gram_of(absorbed.reshape(RK * points_local, rank_right)), ('gx',...  229 us
    another operation x7, other arithmetic, per_device(): factor = jnp.linalg.cholesky(summed / (RK * total_points)).T  34.7 us
    another operation x6, other arithmetic, per_device(): jnp.linalg.cholesky(lax.psum(gram_of(unfold), ('gx', 'gy', 'gz')))  34.1 us
    dot_general x2, matrix products, gram_of(): lax.dot_general(matrix_rows, matrix_rows, (((0,), (0,)), ((), ())), preci...  17.3 us
  transfers between devices with their start and end apart: 2, of which 2 were waited for; matrix products, arithmetic and copies ran while one was open for 4% of the time, Pallas kernels for 0%

commit v1 on v0

--- a/solution.py
+++ b/solution.py
@@ -36,7 +36,8 @@
         precision=lax.Precision.HIGHEST,
         preferred_element_type=jnp.float32,
     )
-    summed = lax.psum(gram_of(absorbed.reshape(RK * points_local, rank_right)), ("gx", "gy", "gz"))
+    half = lax.psum(gram_of(absorbed.reshape(RK * points_local, rank_right)), "gx")
+    summed = lax.psum(half, ("gy", "gz"))
     factor = jnp.linalg.cholesky(summed / (RK * total_points)).T
     right_out = absorbed.reshape(RK, points_local, rank_right)
     return (left_out, right_out, factor)

time: 623 us -> 585 us (0.939)
  waiting for transfers between devices: 474 us -> 439 us
    psum x1 -> x2, waiting for transfers between devices: 229 us -> 194 us  [the longest x1 144 us: per_device(): summed = lax.psum(half, ('gy', 'gz'))]
  transfers between devices with their start and end apart: 2 -> 3, of which waited for: 2 -> 3; matrix products, arithmetic and copies ran while one was open for 4% -> 4% of each run, Pallas kernels for 0% -> 0%
where the time goes in v1:
time: 585 us; the launch traced here: 579 us
  waiting for transfers between devices  439 us (75%)
  other arithmetic  81.6 us (14%)
  matrix products  26.2 us (4%)
  between operations  16.8 us (3%)
  local copies, waits for them, and re-layouts  15.5 us (3%)
    psum x1, waiting for transfers between devices, per_device(): lax.psum(gram_of(unfold), ('gx', 'gy', 'gz'))  245 us
    psum x1, waiting for transfers between devices, per_device(): summed = lax.psum(half, ('gy', 'gz'))  144 us
    psum x1, waiting for transfers between devices, per_device(): lax.psum(gram_of(absorbed.reshape(RK * points_local, rank_right)), 'gx')  49.7 us
    another operation x7, other arithmetic, per_device(): factor = jnp.linalg.cholesky(summed / (RK * total_points)).T  34.7 us
    another operation x6, other arithmetic, per_device(): jnp.linalg.cholesky(lax.psum(gram_of(unfold), ('gx', 'gy', 'gz')))  34.1 us
    dot_general x2, matrix products, gram_of(): lax.dot_general(matrix_rows, matrix_rows, (((0,), (0,)), ((), ())), preci...  17.3 us
  transfers between devices with their start and end apart: 3, of which 3 were waited for; matrix products, arithmetic and copies ran while one was open for 4% of the time, Pallas kernels for 0%

profile of v1, /device:TPU:2, one launch (start us, length us, event | category | flops | bytes accessed | tf_op | source)
XLA Modules:
  0.0 579.2 jit_solution(320095401093729599)
XLA Ops:
  7.2 0.0 all-reduce.5.cloned.1.call-start
  7.2 10.9 %convolution_bitcast_fusion = f32[256,256]{0,1:T(8,128)} fusion(f32[256,16,256]{2,1,0:T(8,128)} %param.3), kind=kOutput, calls=%fused_computation.3 | convolution fusion | flops 3221225472 | bytes 4456448 | tf_op jit(solution)/shard_map/dot_general | solution.py:11
  18.1 0.0 all-reduce.5.cloned.1.call-update
  18.1 0.5 all-reduce.7.cloned.1.call-start
  18.6 7.9 %copy.26 = f32[32,8,16,256]{3,1,2,0:T(8,128)} copy(f32[32,8,16,256]{3,2,1,0:T(8,128)} %bitcast.53) | data formatting | bytes 8388608
  26.5 244.9 %all-reduce.5.cloned.1.call-done = f32[256,256]{0,1:T(8,128)} async-done(((f32[256,256]{0,1:T(8,128)}), f32[256,256]{0,1:T(8,128)}) %all-reduce.5.cloned.1.call-update) | async-done | bytes 262160 | tf_op jit(solution)/shard_map/psum | solution.py:25
  271.5 1.1 copy.16
  272.6 1.0 fusion.3
  273.6 11.7 %cholesky.130 = f32[128,128]{1,0:T(8,128)S(1)} custom-call(f32[128,128]{1,0:T(8,128)S(1)} %cholesky.194), custom_call_target="Cholesky" | custom-call | tf_op jit(solution)/shard_map/jit(cholesky)/cholesky | solution.py:25
  285.3 9.8 %custom-call.13 = f32[1,128,128]{1,2,0:T(8,128)S(1)} custom-call(f32[1,128,128]{2,1,0:T(8,128)S(1)} %get-tuple-element.17), custom_call_target="InvertDiagBlocksLowerTriangular" | custom-call | tf_op jit(solution)/shard_map/jit(cholesky)/cholesky | solution.py:25
  295.2 0.2 constant_dynamic-update-slice_fusion.3
  295.4 0.3 convolution_subtract_fusion.1
  295.6 11.9 %cholesky.147 = f32[128,128]{1,0:T(8,128)S(1)} custom-call(f32[128,128]{1,0:T(8,128)S(1)} %convolution_subtract_fusion.1), custom_call_target="Cholesky" | custom-call | tf_op jit(solution)/shard_map/jit(cholesky)/cholesky | solution.py:25
  307.5 0.6 compare_reduce_fusion.2
  309.6 4.5 fusion.4
  314.1 1.5 reshape.39
  315.5 6.4 %fusion.14 = f32[256,256]{0,1:T(8,128)} fusion(f32[2048,256]{1,0:T(8,128)} %reshape.39), kind=kOutput, calls=%fused_computation.41 | convolution fusion | flops 1610612736 | bytes 2359296 | tf_op jit(solution)/shard_map/dot_general | solution.py:11
  321.9 0.0 all-reduce.7.cloned.1.call-update
  321.9 0.0 all-reduce.9.cloned.1.call-start
  322.0 2.0 copy.27
  324.0 9.8 %custom-call.11 = f32[1,128,128]{1,2,0:T(8,128)S(1)} custom-call(f32[1,128,128]{2,1,0:T(8,128)S(1)} %fusion.8), custom_call_target="InvertDiagBlocksLowerTriangular" | custom-call | tf_op jit(solution)/shard_map/triangular_solve | solution.py:27
  333.8 49.7 %all-reduce.7.cloned.1.call-done = f32[256,256]{0,1:T(8,128)} async-done(((f32[256,256]{0,1:T(8,128)}), f32[256,256]{0,1:T(8,128)}) %all-reduce.7.cloned.1.call-update) | async-done | bytes 262160 | tf_op jit(solution)/shard_map/psum | solution.py:39
  383.5 0.0 all-reduce.9.cloned.1.call-update
  383.5 3.5 fusion
  387.0 2.0 copy.17
  389.1 143.9 %all-reduce.9.cloned.1.call-done = f32[256,256]{0,1:T(8,128)} async-done(((f32[256,256]{0,1:T(8,128)}), f32[256,256]{0,1:T(8,128)}) %all-reduce.9.cloned.1.call-update) | async-done | bytes 262160 | tf_op jit(solution)/shard_map/psum | solution.py:40
  532.9 1.0 broadcast_multiply_fusion
  533.9 0.1 copy.19
  534.0 1.0 fusion.2
  535.1 11.7 %cholesky.164 = f32[128,128]{1,0:T(8,128)S(1)} custom-call(f32[128,128]{1,0:T(8,128)S(1)} %cholesky.197), custom_call_target="Cholesky" | custom-call | tf_op jit(solution)/shard_map/jit(cholesky)/cholesky | solution.py:41
  546.8 9.8 %custom-call.14 = f32[1,128,128]{1,2,0:T(8,128)S(1)} custom-call(f32[1,128,128]{2,1,0:T(8,128)S(1)} %get-tuple-element.13), custom_call_target="InvertDiagBlocksLowerTriangular" | custom-call | tf_op jit(solution)/shard_map/jit(cholesky)/cholesky | solution.py:41
  556.6 0.2 constant_dynamic-update-slice_fusion.1
  556.9 0.3 convolution_subtract_fusion
  557.1 11.7 %cholesky.181 = f32[128,128]{1,0:T(8,128)S(1)} custom-call(f32[128,128]{1,0:T(8,128)S(1)} %convolution_subtract_fusion), custom_call_target="Cholesky" | custom-call | tf_op jit(solution)/shard_map/jit(cholesky)/cholesky | solution.py:41
  568.9 0.7 compare_reduce_fusion
  569.6 0.6 compare_reduce_fusion.1
  571.6 0.8 copy.20
  (12 shorter events, 0.3 us)
Async XLA Ops:
  7.2 264.3 %all-reduce.5.cloned.1.call-start = ((), (), s32[]{:S(2)}) async-start(), calls=%async_computation | async-start | bytes 524288 | tf_op jit(solution)/shard_map/psum | solution.py:25
  18.1 365.4 %all-reduce.7.cloned.1.call-start = ((), (), s32[]{:S(2)}) async-start(), calls=%async_computation.1 | async-start | bytes 524288 | tf_op jit(solution)/shard_map/psum | solution.py:39
  321.9 211.0 %all-reduce.9.cloned.1.call-start = ((), (), s32[]{:S(2)}) async-start(), calls=%async_computation.2 | async-start | bytes 524288 | tf_op jit(solution)/shard_map/psum | solution.py:40
Sparse Core Ops, SparseCore 0:
  18.2 253.1 all-reduce.4
  322.1 61.3 all-reduce.6
  387.4 145.5 all-reduce.8
